TPU v7x, 32 devices: a whole 2x2x4 slice. The times are simulated.
32 devices in a mesh: wide: 8 (over z, y), narrow: 4 (over x, core).
Axes of the slice: x: 2, y: 2, z: 4, core: 2. Of those that a mesh axis runs over, the one named last changes fastest.
Arguments:
- patches: bfloat16 [128, 256, 768], P(('wide', 'narrow')), may hold values from -6 to 6
- counts: int32 [128], P(('wide', 'narrow')), may hold values from 16 to 256, as said below
- cotangent: bfloat16 [128, 256, 768], P(('wide', 'narrow')), may hold values from -6 to 6
- input_weight: bfloat16 [768, 2304], P(('wide', 'narrow')), may hold values from -0.21875 to 0.21875
- output_weight: bfloat16 [768, 768], P(('wide', 'narrow')), may hold values from -0.875 to 0.875
- expand_weight: bfloat16 [768, 3072], P(('wide', 'narrow')), may hold values from -0.21875 to 0.21875
- reduce_weight: bfloat16 [3072, 768], P(('wide', 'narrow')), may hold values from -0.15625 to 0.15625
- norm1_gain: bfloat16 [768], P(('wide', 'narrow')), may hold values from 0.5 to 1.5
- norm1_shift: bfloat16 [768], P(('wide', 'narrow')), may hold values from -1.75 to 1.75
- query_bias: bfloat16 [768], P(('wide', 'narrow')), may hold values from -3 to 3
- value_bias: bfloat16 [768], P(('wide', 'narrow')), may hold values from -1.75 to 1.75
- output_bias: bfloat16 [768], P(('wide', 'narrow')), may hold values from -1.75 to 1.75
- branch1_scale: bfloat16 [768], P(('wide', 'narrow')), may hold values from 0.29882812 to 1.5
- norm2_gain: bfloat16 [768], P(('wide', 'narrow')), may hold values from 0.5 to 1.5
- norm2_shift: bfloat16 [768], P(('wide', 'narrow')), may hold values from -1.75 to 1.75
- expand_bias: bfloat16 [3072], P(('wide', 'narrow')), may hold values from -3 to 3
- reduce_bias: bfloat16 [768], P(('wide', 'narrow')), may hold values from -1.75 to 1.75
- branch2_scale: bfloat16 [768], P(('wide', 'narrow')), may hold values from 0.29882812 to 1.5
Outputs:
- activations: bfloat16 [128, 256, 768], P(('wide', 'narrow'))
- input_grad: float32 [128, 256, 768], P(('wide', 'narrow'))
- input_weight_grad: float32 [768, 2304], P(('wide', 'narrow'))
- output_weight_grad: float32 [768, 768], P(('wide', 'narrow'))
- expand_weight_grad: float32 [768, 3072], P(('wide', 'narrow'))
- reduce_weight_grad: float32 [3072, 768], P(('wide', 'narrow'))
- norm1_gain_grad: float32 [768], P(('wide', 'narrow'))
- norm1_shift_grad: float32 [768], P(('wide', 'narrow'))
- query_bias_grad: float32 [768], P(('wide', 'narrow'))
- value_bias_grad: float32 [768], P(('wide', 'narrow'))
- output_bias_grad: float32 [768], P(('wide', 'narrow'))
- branch1_scale_grad: float32 [768], P(('wide', 'narrow'))
- norm2_gain_grad: float32 [768], P(('wide', 'narrow'))
- norm2_shift_grad: float32 [768], P(('wide', 'narrow'))
- expand_bias_grad: float32 [3072], P(('wide', 'narrow'))
- reduce_bias_grad: float32 [768], P(('wide', 'narrow'))
- branch2_scale_grad: float32 [768], P(('wide', 'narrow'))
Inputs may be any that keep to these rules, and one draw needn't show every extreme that they name: `counts`: valid patches of each image, heavy-tailed; every draw holds full images and images with only 16 valid patches.
All inputs are finite; a program needn't handle non-finite values.
Results may differ from a plain program's by a relative error of at most 0.015.
Values may be sent and summed in bfloat16 or wider, within the bound.
No kernel may reach another device: no remote copies, remote signals or barrier semaphores. Data moves between devices by JAX's collectives and lax.ppermute only.
A program may use at most 192 MiB of HBM per device.

v0:
```python
from functools import partial
import jax
import jax.numpy as jnp
from jax import lax
from jax.sharding import PartitionSpec as P

HEADS = 12
HEAD = 64


def layer_norm(inputs, norm_gain, norm_shift):
    average = jnp.mean(inputs, axis=-1, keepdims=True)
    centered = inputs - average
    spread = jnp.mean(centered * centered, axis=-1, keepdims=True)
    return centered * lax.rsqrt(spread + 1e-06) * norm_gain + norm_shift


def contract_rows(left, right):
    return lax.dot_general(
        left, right, (((0,), (0,)), ((), ())), preferred_element_type=jnp.float32
    )


def contract_cols(left, right):
    return lax.dot_general(
        left, right, (((1,), (1,)), ((), ())), preferred_element_type=jnp.float32
    )


def column_sum(values):
    return jnp.sum(values.astype(jnp.float32), axis=0)


def regroup(gradient, wide_count, narrow_count):
    total_rows = gradient.shape[0]
    piece_rows = total_rows // (wide_count * narrow_count)
    split = gradient.reshape((wide_count, narrow_count, piece_rows) + gradient.shape[1:])
    return jnp.swapaxes(split, 0, 1).reshape(gradient.shape)


def per_device(
    patches,
    counts,
    cotangent,
    input_weight,
    output_weight,
    expand_weight,
    reduce_weight,
    norm1_gain,
    norm1_shift,
    query_bias,
    value_bias,
    output_bias,
    branch1_scale,
    norm2_gain,
    norm2_shift,
    expand_bias,
    reduce_bias,
    branch2_scale,
):
    whole = (
        lax.all_gather(input_weight, ("wide", "narrow"), axis=0, tiled=True),
        lax.all_gather(output_weight, ("wide", "narrow"), axis=0, tiled=True),
        lax.all_gather(expand_weight, ("wide", "narrow"), axis=0, tiled=True),
        lax.all_gather(reduce_weight, ("wide", "narrow"), axis=0, tiled=True),
        lax.all_gather(norm1_gain, ("wide", "narrow"), axis=0, tiled=True),
        lax.all_gather(norm1_shift, ("wide", "narrow"), axis=0, tiled=True),
        lax.all_gather(query_bias, ("wide", "narrow"), axis=0, tiled=True),
        lax.all_gather(value_bias, ("wide", "narrow"), axis=0, tiled=True),
        lax.all_gather(output_bias, ("wide", "narrow"), axis=0, tiled=True),
        lax.all_gather(branch1_scale, ("wide", "narrow"), axis=0, tiled=True),
        lax.all_gather(norm2_gain, ("wide", "narrow"), axis=0, tiled=True),
        lax.all_gather(norm2_shift, ("wide", "narrow"), axis=0, tiled=True),
        lax.all_gather(expand_bias, ("wide", "narrow"), axis=0, tiled=True),
        lax.all_gather(reduce_bias, ("wide", "narrow"), axis=0, tiled=True),
        lax.all_gather(branch2_scale, ("wide", "narrow"), axis=0, tiled=True),
    )
    w_input, w_output, w_expand, w_reduce = (whole[0], whole[1], whole[2], whole[3])
    (
        gain_one,
        shift_one,
        bias_query,
        bias_value,
        bias_output,
        scale_one,
        gain_two,
        shift_two,
        bias_expand,
        bias_reduce,
        scale_two,
    ) = tuple((item.astype(jnp.float32) for item in whole[4:]))
    n_images, n_patch, width = patches.shape
    n_rows = n_images * n_patch
    head_shape = (n_images, n_patch, HEADS, HEAD)
    score_scale = HEAD ** (-0.5)
    position = jnp.arange(n_patch, dtype=jnp.int32)
    valid_keys = position[None, :] < counts[:, None]
    row_mask = jnp.where(valid_keys, 1.0, 0.0).astype(jnp.float32).reshape(n_rows, 1)
    rows_in = patches.astype(jnp.float32).reshape(n_rows, width)
    normed_low = layer_norm(rows_in, gain_one, shift_one).astype(jnp.bfloat16)
    projections = jnp.dot(normed_low, w_input, preferred_element_type=jnp.float32)
    queries = (projections[:, :width] + bias_query).astype(jnp.bfloat16).reshape(head_shape)
    key_rows = projections[:, width : 2 * width].astype(jnp.bfloat16).reshape(head_shape)
    values = (projections[:, 2 * width :] + bias_value).astype(jnp.bfloat16).reshape(head_shape)

    def attention_scores():
        raw_scores = jnp.einsum(
            "iphd,iqhd->ihpq", queries, key_rows, preferred_element_type=jnp.float32
        )
        return jnp.where(valid_keys[:, None, None, :], raw_scores * score_scale, -1e30)

    scores = attention_scores()
    log_total = jax.nn.logsumexp(scores, axis=-1, keepdims=True)
    soft_low = jnp.exp(scores - log_total).astype(jnp.bfloat16)
    attended = jnp.einsum("ihpq,iqhd->iphd", soft_low, values, preferred_element_type=jnp.float32)
    attended_low = attended.astype(jnp.bfloat16).reshape(n_rows, width)
    projected = jnp.dot(attended_low, w_output, preferred_element_type=jnp.float32) + bias_output
    middle = rows_in + scale_one * projected
    second_low = layer_norm(middle, gain_two, shift_two).astype(jnp.bfloat16)
    hidden = jnp.dot(second_low, w_expand, preferred_element_type=jnp.float32) + bias_expand
    activated_low = jax.nn.gelu(hidden, approximate=False).astype(jnp.bfloat16)
    branch = jnp.dot(activated_low, w_reduce, preferred_element_type=jnp.float32) + bias_reduce
    outputs = middle + scale_two * branch
    again = (
        lax.all_gather(input_weight, ("wide", "narrow"), axis=0, tiled=True),
        lax.all_gather(output_weight, ("wide", "narrow"), axis=0, tiled=True),
        lax.all_gather(expand_weight, ("wide", "narrow"), axis=0, tiled=True),
        lax.all_gather(reduce_weight, ("wide", "narrow"), axis=0, tiled=True),
    )
    back_input, back_output, back_expand, back_reduce = (again[0], again[1], again[2], again[3])
    grad_out = cotangent.astype(jnp.float32).reshape(n_rows, width) * row_mask
    grad_branch = (grad_out * scale_two).astype(jnp.bfloat16)
    grad_scale_two = jnp.sum(grad_out * branch, axis=0)
    grad_bias_reduce = column_sum(grad_branch)
    grad_w_reduce = contract_rows(activated_low, grad_branch)
    grad_activated = contract_cols(grad_branch, back_reduce)
    gelu_exact = partial(jax.nn.gelu, approximate=False)
    _, gelu_back = jax.vjp(gelu_exact, hidden)
    grad_hidden = gelu_back(grad_activated)[0].astype(jnp.bfloat16)
    grad_bias_expand = column_sum(grad_hidden)
    grad_w_expand = contract_rows(second_low, grad_hidden)
    grad_second = contract_cols(grad_hidden, back_expand)
    _, norm_back_two = jax.vjp(layer_norm, middle, gain_two, shift_two)
    grad_middle, grad_gain_two, grad_shift_two = norm_back_two(grad_second)
    grad_middle = grad_middle + grad_out
    grad_projected = (grad_middle * scale_one).astype(jnp.bfloat16)
    grad_scale_one = jnp.sum(grad_middle * projected, axis=0)
    grad_bias_output = column_sum(grad_projected)
    grad_w_output = contract_rows(attended_low, grad_projected)
    grad_attended = (
        contract_cols(grad_projected, back_output).astype(jnp.bfloat16).reshape(head_shape)
    )
    scores = attention_scores()
    soft_full = jnp.exp(scores - log_total)
    soft_again = soft_full.astype(jnp.bfloat16)
    grad_soft = jnp.einsum(
        "iphd,iqhd->ihpq", grad_attended, values, preferred_element_type=jnp.float32
    )
    grad_values = jnp.einsum(
        "ihpq,iphd->iqhd", soft_again, grad_attended, preferred_element_type=jnp.float32
    ).astype(jnp.bfloat16)
    grad_scores = (
        soft_full * (grad_soft - jnp.sum(soft_full * grad_soft, axis=-1, keepdims=True))
    ).astype(jnp.bfloat16)
    grad_queries = (
        (
            jnp.einsum("ihpq,iqhd->iphd", grad_scores, key_rows, preferred_element_type=jnp.float32)
            * score_scale
        )
        .astype(jnp.bfloat16)
        .reshape(n_rows, width)
    )
    grad_keys = (
        (
            jnp.einsum("ihpq,iphd->iqhd", grad_scores, queries, preferred_element_type=jnp.float32)
            * score_scale
        )
        .astype(jnp.bfloat16)
        .reshape(n_rows, width)
    )
    grad_values = grad_values.reshape(n_rows, width)
    grad_bias_query = column_sum(grad_queries)
    grad_bias_value = column_sum(grad_values)
    grad_projections = jnp.concatenate([grad_queries, grad_keys, grad_values], axis=1)
    grad_w_input = contract_rows(normed_low, grad_projections)
    grad_normed = contract_cols(grad_projections, back_input)
    _, norm_back_one = jax.vjp(layer_norm, rows_in, gain_one, shift_one)
    grad_rows, grad_gain_one, grad_shift_one = norm_back_one(grad_normed)
    input_grad = grad_rows + grad_middle
    wide_count = lax.axis_size("wide")
    narrow_count = lax.axis_size("narrow")
    (
        part_w_input,
        part_w_output,
        part_w_expand,
        part_w_reduce,
        part_gain_one,
        part_shift_one,
        part_bias_query,
        part_bias_value,
        part_bias_output,
        part_scale_one,
        part_gain_two,
        part_shift_two,
        part_bias_expand,
        part_bias_reduce,
        part_scale_two,
    ) = tuple(
        (
            regroup(item, wide_count, narrow_count)
            for item in (
                grad_w_input,
                grad_w_output,
                grad_w_expand,
                grad_w_reduce,
                grad_gain_one,
                grad_shift_one,
                grad_bias_query,
                grad_bias_value,
                grad_bias_output,
                grad_scale_one,
                grad_gain_two,
                grad_shift_two,
                grad_bias_expand,
                grad_bias_reduce,
                grad_scale_two,
            )
        )
    )
    inner = (
        lax.psum_scatter(
            part_w_input.astype(jnp.bfloat16), "narrow", scatter_dimension=0, tiled=True
        ).astype(jnp.float32),
        lax.psum_scatter(
            part_w_output.astype(jnp.bfloat16), "narrow", scatter_dimension=0, tiled=True
        ).astype(jnp.float32),
        lax.psum_scatter(
            part_w_expand.astype(jnp.bfloat16), "narrow", scatter_dimension=0, tiled=True
        ).astype(jnp.float32),
        lax.psum_scatter(
            part_w_reduce.astype(jnp.bfloat16), "narrow", scatter_dimension=0, tiled=True
        ).astype(jnp.float32),
        lax.psum_scatter(
            part_gain_one.astype(jnp.bfloat16), "narrow", scatter_dimension=0, tiled=True
        ).astype(jnp.float32),
        lax.psum_scatter(
            part_shift_one.astype(jnp.bfloat16), "narrow", scatter_dimension=0, tiled=True
        ).astype(jnp.float32),
        lax.psum_scatter(
            part_bias_query.astype(jnp.bfloat16), "narrow", scatter_dimension=0, tiled=True
        ).astype(jnp.float32),
        lax.psum_scatter(
            part_bias_value.astype(jnp.bfloat16), "narrow", scatter_dimension=0, tiled=True
        ).astype(jnp.float32),
        lax.psum_scatter(
            part_bias_output.astype(jnp.bfloat16), "narrow", scatter_dimension=0, tiled=True
        ).astype(jnp.float32),
        lax.psum_scatter(
            part_scale_one.astype(jnp.bfloat16), "narrow", scatter_dimension=0, tiled=True
        ).astype(jnp.float32),
        lax.psum_scatter(
            part_gain_two.astype(jnp.bfloat16), "narrow", scatter_dimension=0, tiled=True
        ).astype(jnp.float32),
        lax.psum_scatter(
            part_shift_two.astype(jnp.bfloat16), "narrow", scatter_dimension=0, tiled=True
        ).astype(jnp.float32),
        lax.psum_scatter(
            part_bias_expand.astype(jnp.bfloat16), "narrow", scatter_dimension=0, tiled=True
        ).astype(jnp.float32),
        lax.psum_scatter(
            part_bias_reduce.astype(jnp.bfloat16), "narrow", scatter_dimension=0, tiled=True
        ).astype(jnp.float32),
        lax.psum_scatter(
            part_scale_two.astype(jnp.bfloat16), "narrow", scatter_dimension=0, tiled=True
        ).astype(jnp.float32),
    )
    summed = (
        lax.psum_scatter(inner[0], "wide", scatter_dimension=0, tiled=True),
        lax.psum_scatter(inner[1], "wide", scatter_dimension=0, tiled=True),
        lax.psum_scatter(inner[2], "wide", scatter_dimension=0, tiled=True),
        lax.psum_scatter(inner[3], "wide", scatter_dimension=0, tiled=True),
        lax.psum_scatter(inner[4], "wide", scatter_dimension=0, tiled=True),
        lax.psum_scatter(inner[5], "wide", scatter_dimension=0, tiled=True),
        lax.psum_scatter(inner[6], "wide", scatter_dimension=0, tiled=True),
        lax.psum_scatter(inner[7], "wide", scatter_dimension=0, tiled=True),
        lax.psum_scatter(inner[8], "wide", scatter_dimension=0, tiled=True),
        lax.psum_scatter(inner[9], "wide", scatter_dimension=0, tiled=True),
        lax.psum_scatter(inner[10], "wide", scatter_dimension=0, tiled=True),
        lax.psum_scatter(inner[11], "wide", scatter_dimension=0, tiled=True),
        lax.psum_scatter(inner[12], "wide", scatter_dimension=0, tiled=True),
        lax.psum_scatter(inner[13], "wide", scatter_dimension=0, tiled=True),
        lax.psum_scatter(inner[14], "wide", scatter_dimension=0, tiled=True),
    )
    return (
        outputs.reshape(n_images, n_patch, width).astype(jnp.bfloat16),
        input_grad.reshape(n_images, n_patch, width),
        summed[0],
        summed[1],
        summed[2],
        summed[3],
        summed[4],
        summed[5],
        summed[6],
        summed[7],
        summed[8],
        summed[9],
        summed[10],
        summed[11],
        summed[12],
        summed[13],
        summed[14],
    )


def solution(mesh):
    placed = (
        P(("wide", "narrow"), None, None),
        P(("wide", "narrow")),
        P(("wide", "narrow"), None, None),
        P(("wide", "narrow"), None),
        P(("wide", "narrow"), None),
        P(("wide", "narrow"), None),
        P(("wide", "narrow"), None),
        P(("wide", "narrow")),
        P(("wide", "narrow")),
        P(("wide", "narrow")),
        P(("wide", "narrow")),
        P(("wide", "narrow")),
        P(("wide", "narrow")),
        P(("wide", "narrow")),
        P(("wide", "narrow")),
        P(("wide", "narrow")),
        P(("wide", "narrow")),
        P(("wide", "narrow")),
    )
    return jax.shard_map(
        per_device,
        mesh=mesh,
        in_specs=placed,
        out_specs=(
            P(("wide", "narrow"), None, None),
            P(("wide", "narrow"), None, None),
            P(("wide", "narrow"), None),
            P(("wide", "narrow"), None),
            P(("wide", "narrow"), None),
            P(("wide", "narrow"), None),
            P(("wide", "narrow")),
            P(("wide", "narrow")),
            P(("wide", "narrow")),
            P(("wide", "narrow")),
            P(("wide", "narrow")),
            P(("wide", "narrow")),
            P(("wide", "narrow")),
            P(("wide", "narrow")),
            P(("wide", "narrow")),
            P(("wide", "narrow")),
            P(("wide", "narrow")),
        ),
        check_vma=False,
    )
```

profile of v0, /device:TPU:0, one launch (start us, length us, event | category | flops | bytes accessed | tf_op | source)
XLA Modules:
  0.0 793.1 jit_solution(13559499145613062602)
XLA Ops:
  25.2 43.4 %all-reduce.34 = (bf16[768]{0:T(1024)(128)(2,1)S(1)}, bf16[768]{0:T(1024)(128)(2,1)S(1)}, bf16[768]{0:T(1024)(128)(2,1)S(1)}, bf16[768]{0:T(1024)(128)(2,1)S(1)}...) all-reduce(bf16[768]{0:T(1024)(128)(2,1)S(1)} %dynamic-update-slice, ...), channel_id=1, replica_groups=mesh['wide'=8,'narrow'=4] {'wide','narrow'}, use_global_device_ids=true, to_apply=%add.2 | all-reduce | flops 10752 | bytes 43008
  70.6 2.6 copy.142
  74.8 6.3 fusion.90
  85.8 2.9 reshape.301
  88.7 3.2 copy.121
  91.9 3.9 reshape.302
  95.8 2.6 copy.119
  98.4 3.9 reshape.300
  102.2 4.5 fusion.23
  106.8 3.9 exponential_reduce_fusion
  111.5 3.5 fusion.51
  116.7 12.8 %all-gather.7.cloned.1.call-done = bf16[768,768]{1,0:T(8,128)(2,1)} async-done(((bf16[24,768]{1,0:T(8,128)(2,1)}), bf16[768,768]{1,0:T(8,128)(2,1)}) %all-gather.7.cloned.1.call-update) | async-done | bytes 1179664 | tf_op jit(solution)/shard_map/all_gather | solution.py:63
  129.5 4.6 fusion.86
  136.4 58.6 %all-gather.9.cloned.1.call-done = bf16[768,3072]{1,0:T(8,128)(2,1)} async-done(((bf16[24,3072]{1,0:T(8,128)(2,1)}), bf16[768,3072]{1,0:T(8,128)(2,1)}) %all-gather.9.cloned.1.call-update) | async-done | bytes 4718608 | tf_op jit(solution)/shard_map/all_gather | solution.py:64
  194.9 36.6 %fusion = (f32[1024,3072]{1,0:T(8,128)}, f32[1024,3072]{1,0:T(8,128)}) fusion(f32[3072]{0:T(1024)S(1)} %convert_element_type.344, bf16[768,3072]{1,0:T(8,128)(2,1)} %all-gather.9.cloned.1.call-done, f32[1024,768]{1,0:T(8,128)} %copy-done.8, f32[768]{0:T(1024)S(1)} %convert_element_type.342, f32[768]{0:T(1024)S(1)} %convert_element_type.341, ...), kind=kOutput, calls=%fused_computation.2 | convolution fusion | flops 5033951232 | bytes 33056768 | tf_op jit(solution)/shard_map/dot_general | solution.py:120
  231.5 28.1 %all-gather.11.cloned.1.call-done = bf16[3072,768]{1,0:T(8,128)(2,1)} async-done(((bf16[96,768]{1,0:T(8,128)(2,1)}), bf16[3072,768]{1,0:T(8,128)(2,1)}) %all-gather.11.cloned.1.call-update) | async-done | bytes 4718608 | tf_op jit(solution)/shard_map/all_gather | solution.py:65
  259.7 16.9 %fusion.89 = (bf16[3072]{0:T(1024)(128)(2,1)S(1)}, bf16[1024,3072]{1,0:T(8,128)(2,1)}) fusion(f32[1024,3072]{1,0:T(8,128)} %get-tuple-element.78, bf16[1024,768]{1,0:T(8,128)(2,1)S(1)} %copy-done.15, bf16[3072,768]{1,0:T(8,128)(2,1)} %all-gather.11.cloned.1.call-done, f32[1024,3072]{1,0:T(8,128)} %get-tuple-element.79, f32[3072]{0:T(1024)S(1)} %convert_element_type.344), kind=kOutput, calls=%fused_computation.157 | convolution fusion | flops 4882166784 | bytes 37767168 | tf_op jit(solution)/shard_map/dot_general | solution.py:25
  276.5 9.4 %multiply_reduce_fusion.2 = (bf16[768]{0:T(1024)(128)(2,1)S(1)}, f32[1024]{0:T(1024)S(1)}, bf16[768]{0:T(1024)(128)(2,1)S(1)}, f32[1024,768]{1,0:T(8,128)S(1)}) fusion(f32[1024,768]{1,0:T(8,128)S(1)} %copy-done.9, f32[1024]{0:T(1024)S(1)} %fusion.70, f32[1024]{0:T(1024)S(1)} %broadcast_multiply_fusion, f32[768]{0:T(1024)S(1)} %convert_element_type.341, ...), kind=kOutput, calls=%fused_computation.80 | convolution fusion | flops 4838126592 | bytes 17319936 | tf_op jit(solution)/shard_map/dot_general | solution.py:25
  292.6 4.3 convolution_convert_fusion.4
  296.9 3.0 copy.127
  300.0 3.9 reshape.305
  303.8 11.0 %multiply_reduce_fusion = (f32[4,12,256]{2,1,0:T(8,128)S(1)}, f32[4,12,256,256]{2,3,1,0:T(8,128)}) fusion(f32[4,12,256,256]{2,3,1,0:T(8,128)} %copy-done, f32[4,12,256]{2,1,0:T(8,128)S(1)} %log_add_fusion, pred[4,256]{1,0:T(4,128)(4,1)S(1)} %iota_compare_fusion, bf16[4,256,12,64]{1,0,3,2:T(4,128)(2,1)S(1)} %copy-done.12, bf16[4,256,12,64]{1,0,3,2:T(4,128)(2,1)} %reshape.305), kind=kOutput, calls=%fused_computation.24 | convolution fusion | flops 418369536 | bytes 28410880 | tf_op jit(solution)/shard_map/iphd,iqhd->ihpq/dot_general | solution.py:156
  314.8 13.4 %multiply_convert_fusion = bf16[4,12,256,256]{2,3,1,0:T(8,128)(2,1)} fusion(f32[4,12,256,256]{2,3,1,0:T(8,128)} %get-tuple-element.82, f32[4,12,256,256]{2,3,1,0:T(8,128)} %copy-done, f32[4,12,256]{2,1,0:T(8,128)S(1)} %get-tuple-element.81, f32[4,12,256]{2,1,0:T(8,128)S(1)} %log_add_fusion, pred[4,256]{1,0:T(4,128)(4,1)S(1)} %iota_compare_fusion), kind=kLoop, calls=%fused_computation.23 | loop fusion | flops 18874368 | bytes 31556608 | tf_op jit(solution)/shard_map/convert_element_type | solution.py:164
  328.3 3.4 fusion.88
  334.4 2.6 copy.141
  337.0 4.8 fusion.54
  344.6 2.8 copy.140
  347.4 4.1 fusion.87
  355.9 6.7 fusion.29
  364.8 9.0 %convolution_convert_fusion = bf16[768,3072]{1,0:T(8,128)(2,1)S(1)} fusion(bf16[1024,3072]{1,0:T(8,128)(2,1)} %get-tuple-element.89, f32[1024,768]{1,0:T(8,128)} %copy-done.8, f32[768]{0:T(1024)S(1)} %convert_element_type.342, f32[768]{0:T(1024)S(1)} %convert_element_type.341, f32[1024]{0:T(1024)S(1)} %fusion.70, f32[1024]{0:T(1024)S(1)} %broadcast_multiply_fusion), kind=kOutput, calls=%fused_computation.50 | convolution fusion | flops 4838129664 | bytes 14170112 | tf_op jit(solution)/shard_map/dot_general | solution.py:19
  373.7 2.5 copy.145
  377.5 30.5 %fusion.3 = bf16[3072,1024]{0,1:T(8,128)(2,1)} fusion(f32[1024,3072]{1,0:T(8,128)} %get-tuple-element.79, f32[3072]{0:T(1024)S(1)} %convert_element_type.344), kind=kLoop, calls=%fused_computation.5 | loop fusion | flops 207618048 | bytes 18886656 | tf_op jit(solution)/shard_map/convert_element_type | solution.py:121
  408.0 8.9 %copy.146 = bf16[3072,1024]{1,0:T(8,128)(2,1)} copy(bf16[3072,1024]{0,1:T(8,128)(2,1)} %fusion.3) | data formatting | bytes 12582912 | tf_op jit(solution)/shard_map/convert_element_type | solution.py:121
  417.0 8.4 %convert_bitcast_fusion = bf16[4,8,96,768]{3,2,0,1:T(8,128)(2,1)S(1)} fusion(bf16[8,4,96,1024]{3,2,1,0:T(8,128)(2,1)} %bitcast.228, bf16[1024,768,1,1]{1,0,3,2:T(8,128)(2,1)S(1)} %bitcast.242), kind=kOutput, calls=%fused_computation.56 | convolution fusion | flops 4834197504 | bytes 12582912 | tf_op jit(solution)/shard_map/dot_general | solution.py:19
  425.4 2.5 copy.147
  430.0 2.6 convert_element_type.364
  432.6 21.4 %reduce-scatter.17.cloned.1.call-done = bf16[192,3072]{1,0:T(8,128)(2,1)} async-done(((bf16[768,3072]{1,0:T(8,128)(2,1)}), bf16[192,3072]{1,0:T(8,128)(2,1)}) %reduce-scatter.17.cloned.1.call-update) | async-done | bytes 1179664 | tf_op jit(solution)/shard_map/reduce_scatter | solution.py:237
  454.1 2.9 convert_element_type.373
  461.1 10.3 %fusion.82 = (bf16[768]{0:T(1024)(128)(2,1)S(1)}, f32[1024]{0:T(1024)S(1)}, f32[1024,768]{1,0:T(8,128)}) fusion(f32[768]{0:T(1024)S(1)} %copy-done.24, f32[1024]{0:T(1024)S(1)} %bitcast.244, bf16[4,256,768]{2,1,0:T(8,128)(2,1)S(1)} %copy-done.2, bf16[768,2304]{1,0:T(8,128)(2,1)} %all-gather.5.cloned.1.call-done, bf16[1024,768]{1,0:T(8,128)(2,1)} %copy.141, ...), kind=kOutput, calls=%fused_computation.150 | convolution fusion | flops 3642751232 | bytes 12988928 | tf_op jit(solution)/shard_map/dot_general | solution.py:25
  471.5 33.1 %reduce-scatter.21.cloned.1.call-done = bf16[768,768]{1,0:T(8,128)(2,1)} async-done(((bf16[3072,768]{1,0:T(8,128)(2,1)}), bf16[768,768]{1,0:T(8,128)(2,1)}) %reduce-scatter.21.cloned.1.call-update) | async-done | bytes 1179664 | tf_op jit(solution)/shard_map/reduce_scatter | solution.py:240
  504.6 2.9 convert_element_type.380
  507.5 3.2 fusion.41
  512.1 20.1 %multiply_reduce_fusion.1 = (bf16[768]{0:T(1024)(128)(2,1)S(1)}, bf16[768]{0:T(1024)(128)(2,1)S(1)}, f32[1024,768]{1,0:T(8,128)}, bf16[1024,768]{1,0:T(8,128)(2,1)}) fusion(bf16[4,256,768]{2,1,0:T(8,128)(2,1)S(1)} %copy-done.6, f32[1024]{0:T(1024)S(1)} %bitcast.249, f32[768]{0:T(1024)S(1)} %convert_element_type.346, f32[1024,768]{1,0:T(8,128)} %get-tuple-element.77, ...), kind=kOutput, calls=%fused_computation.79 | convolution fusion | flops 4861720576 | bytes 50383872 | tf_op jit(solution)/shard_map/dot_general | solution.py:122
  532.9 10.9 %all-reduce.35 = (bf16[768]{0:T(1024)(128)(2,1)S(1)}, bf16[768]{0:T(1024)(128)(2,1)S(1)}, bf16[768]{0:T(1024)(128)(2,1)S(1)}, bf16[768]{0:T(1024)(128)(2,1)S(1)}...) all-reduce(bf16[768]{0:T(1024)(128)(2,1)S(1)} %convert_element_type, ...), channel_id=10, replica_groups=mesh['wide'=8,'narrow'=4] {'narrow'}, use_global_device_ids=true, to_apply=%region_20.21.clone | all-reduce | flops 10752 | bytes 43008
  544.2 36.8 %all-reduce.33 = (f32[192]{0:T(256)S(1)}, f32[192]{0:T(256)S(1)}, f32[192]{0:T(256)S(1)}, f32[192]{0:T(256)S(1)}, f32[192]{0:T(256)S(1)}, /*index=5*/f32[192]{0:...) all-reduce(f32[192]{0:T(256)S(1)} %get-tuple-element.99, ...), channel_id=11, replica_groups=mesh['wide'=8,'narrow'=4] {'wide'}, use_global_device_ids=true, to_apply=%region_21.22.clone | all-reduce | flops 2688 | bytes 21504
  587.4 53.4 %reduce-scatter.11.cloned.1.call-done = f32[24,2304]{1,0:T(8,128)} async-done(((f32[192,2304]{1,0:T(8,128)}), f32[24,2304]{1,0:T(8,128)}) %reduce-scatter.11.cloned.1.call-update) | async-done | bytes 221200 | tf_op jit(solution)/shard_map/reduce_scatter | solution.py:278
  640.7 72.5 %reduce-scatter.19.cloned.1.call-done = f32[24,3072]{1,0:T(8,128)} async-done(((f32[192,3072]{1,0:T(8,128)}), f32[24,3072]{1,0:T(8,128)}) %reduce-scatter.19.cloned.1.call-update) | async-done | bytes 294928 | tf_op jit(solution)/shard_map/reduce_scatter | solution.py:280
  713.3 72.8 %reduce-scatter.23.cloned.1.call-done = f32[96,768]{1,0:T(8,128)} async-done(((f32[768,768]{1,0:T(8,128)}), f32[96,768]{1,0:T(8,128)}) %reduce-scatter.23.cloned.1.call-update) | async-done | bytes 294928 | tf_op jit(solution)/shard_map/reduce_scatter | solution.py:281
  (234 shorter events, 62.8 us)
Async XLA Ops:
  7.2 61.6 %copy-start.1 = (bf16[4,256,768]{2,1,0:T(8,128)(2,1)S(1)}, bf16[4,256,768]{2,1,0:T(8,128)(2,1)}, u32[]{:S(2)}) copy-start(bf16[4,256,768]{2,1,0:T(8,128)(2,1)} %param.18) | copy-start | bytes 4718596
  7.2 67.6 %all-gather.5.cloned.1.call-start = ((), (), s32[]{:S(2)}) async-start(), calls=%async_computation.8 | async-start | bytes 3649536 | tf_op jit(solution)/shard_map/all_gather | solution.py:62
  7.9 121.6 %all-gather.7.cloned.1.call-start = ((), (), s32[]{:S(2)}) async-start(), calls=%async_computation.9 | async-start | bytes 1216512 | tf_op jit(solution)/shard_map/all_gather | solution.py:63
  8.7 186.3 %all-gather.9.cloned.1.call-start = ((), (), s32[]{:S(2)}) async-start(), calls=%async_computation.10 | async-start | bytes 4866048 | tf_op jit(solution)/shard_map/all_gather | solution.py:64
  9.4 250.2 %all-gather.11.cloned.1.call-start = ((), (), s32[]{:S(2)}) async-start(), calls=%async_computation.11 | async-start | bytes 4866048 | tf_op jit(solution)/shard_map/all_gather | solution.py:65
  10.0 418.0 %reduce-scatter.13.cloned.1.call-start = ((), (), s32[]{:S(2)}) async-start(), calls=%async_computation.14 | async-start | bytes 1474560 | tf_op jit(solution)/shard_map/reduce_scatter | solution.py:234
  12.1 61.1 %copy-start.5 = (bf16[4,256,768]{2,1,0:T(8,128)(2,1)S(1)}, bf16[4,256,768]{2,1,0:T(8,128)(2,1)}, u32[]{:S(2)}) copy-start(bf16[4,256,768]{2,1,0:T(8,128)(2,1)} %param.20) | copy-start | bytes 4718596
  13.9 60.8 %copy-start.19 = (f32[1,2,4,128]{3,1,2,0:T(2,128)}, f32[1,2,4,128]{3,1,2,0:T(2,128)S(1)}, u32[]{:S(2)}) copy-start(f32[1,2,4,128]{3,1,2,0:T(2,128)S(1)} %copy.166) | copy-start | bytes 12292
  15.9 52.7 %copy-start.29 = (f32[1,2,4,128]{3,1,2,0:T(2,128)}, f32[1,2,4,128]{3,1,2,0:T(2,128)S(1)}, u32[]{:S(2)}) copy-start(f32[1,2,4,128]{3,1,2,0:T(2,128)S(1)} %copy.167) | copy-start | bytes 12292
  16.0 58.8 %copy-start.21 = (f32[1024]{0:T(1024)}, f32[1024]{0:T(1024)S(1)}, u32[]{:S(2)}) copy-start(f32[1024]{0:T(1024)S(1)} %rsqrt.22) | copy-start | bytes 12292
  68.6 6.1 copy-start.23
  68.7 6.1 copy-start.25
  68.7 60.8 %copy-start.32 = (f32[768]{0:T(1024)}, f32[768]{0:T(1024)S(1)}, u32[]{:S(2)}) copy-start(f32[768]{0:T(1024)S(1)} %convert_element_type.339) | copy-start | bytes 9220
  68.7 6.0 copy-start.27
  88.7 13.5 %copy-start.3 = (bf16[4,256,12,64]{1,0,3,2:T(4,128)(2,1)}, bf16[4,256,12,64]{1,0,3,2:T(4,128)(2,1)S(1)}, u32[]{:S(2)}) copy-start(bf16[4,256,12,64]{1,0,3,2:T(4,128)(2,1)S(1)} %reshape.301) | copy-start | bytes 4718596
  106.8 4.7 copy-start
  106.8 4.7 copy-start.11
  116.7 17.5 %copy-start.16 = (bf16[96,8,4,256]{3,1,2,0:T(8,128)(2,1)}, bf16[96,8,4,256]{3,1,2,0:T(8,128)(2,1)S(1)}, u32[]{:S(2)}) copy-start(bf16[96,8,4,256]{3,1,2,0:T(8,128)(2,1)S(1)} %copy.168) | copy-start | bytes 4718596
  134.1 1.7 copy-start.8
  136.4 123.3 %copy-start.15 = (bf16[1024,768]{1,0:T(8,128)(2,1)S(1)}, bf16[1024,768]{1,0:T(8,128)(2,1)}, u32[]{:S(2)}) copy-start(bf16[1024,768]{1,0:T(8,128)(2,1)} %multiply_convert_fusion.7) | copy-start | bytes 4718596
  259.7 16.9 %copy-start.9 = (f32[1024,768]{1,0:T(8,128)S(1)}, f32[1024,768]{1,0:T(8,128)}, u32[]{:S(2)}) copy-start(f32[1024,768]{1,0:T(8,128)} %copy-done.8) | copy-start | bytes 9437188
  287.4 4.0 copy-start.10
  287.4 2.6 copy-start.17
  288.2 4.3 copy-start.18
  292.6 137.4 %reduce-scatter.9.cloned.1.call-start = ((), (), s32[]{:S(2)}) async-start(), calls=%async_computation.12 | async-start | bytes 4423680 | tf_op jit(solution)/shard_map/reduce_scatter | solution.py:231
  296.9 6.9 copy-start.12
  303.8 24.4 %slice-start = ((s8[12582912]{0:T(1024)(128)(4,1)}), s8[4194304]{0:T(1024)(128)(4,1)S(1)}, s32[]{:S(2)}) async-start(s8[12582912]{0:T(1024)(128)(4,1)} %bitcast.223), calls=%async_computation.20 | async-start | bytes 8388608
  303.8 24.4 %slice-start.1 = ((s8[12582912]{0:T(1024)(128)(4,1)}), s8[4194304]{0:T(1024)(128)(4,1)S(1)}, s32[]{:S(2)}) async-start(s8[12582912]{0:T(1024)(128)(4,1)} %bitcast.223), calls=%async_computation.21 | async-start | bytes 8388608
  314.8 13.4 %slice-start.2 = ((s8[12582912]{0:T(1024)(128)(4,1)}), s8[4194304]{0:T(1024)(128)(4,1)S(1)}, s32[]{:S(2)}) async-start(s8[12582912]{0:T(1024)(128)(4,1)} %bitcast.223), calls=%async_computation.22 | async-start | bytes 8388608
  314.8 13.4 %copy-start.13 = (bf16[4,256,12,64]{1,0,3,2:T(4,128)(2,1)S(1)}, bf16[4,256,12,64]{1,0,3,2:T(4,128)(2,1)}, u32[]{:S(2)}) copy-start(bf16[4,256,12,64]{1,0,3,2:T(4,128)(2,1)} %reshape.305) | copy-start | bytes 4718596
  331.7 5.3 copy-start.4
  341.8 5.5 copy-start.7
  355.9 6.8 copy-start.14
  364.7 89.4 %reduce-scatter.17.cloned.1.call-start = ((), (), s32[]{:S(2)}) async-start(), calls=%async_computation.16 | async-start | bytes 5898240 | tf_op jit(solution)/shard_map/reduce_scatter | solution.py:237
  376.3 128.3 %reduce-scatter.21.cloned.1.call-start = ((), (), s32[]{:S(2)}) async-start(), calls=%async_computation.18 | async-start | bytes 5898240 | tf_op jit(solution)/shard_map/reduce_scatter | solution.py:240
  427.9 159.5 %reduce-scatter.15.cloned.1.call-start = ((), (), s32[]{:S(2)}) async-start(), calls=%async_computation.15 | async-start | bytes 663552 | tf_op jit(solution)/shard_map/reduce_scatter | solution.py:279
  429.8 27.2 %copy-start.36 = (u32[32]{0:T(128)S(1)}, u32[32]{0:T(128)}, u32[]{:S(2)}) copy-start(u32[32]{0:T(128)} %constant.159) | copy-start | bytes 388
  429.8 29.1 %copy-start.35 = (u32[32]{0:T(128)S(1)}, u32[32]{0:T(128)}, u32[]{:S(2)}) copy-start(u32[32]{0:T(128)} %constant.155) | copy-start | bytes 388
  429.9 31.0 %copy-start.34 = (bf16[768]{0:T(1024)(128)(2,1)S(1)}, bf16[768]{0:T(1024)(128)(2,1)}, u32[]{:S(2)}) copy-start(bf16[768]{0:T(1024)(128)(2,1)} %get-tuple-element.46) | copy-start | bytes 4612
  429.9 31.2 %copy-start.2 = (bf16[4,256,768]{2,1,0:T(8,128)(2,1)S(1)}, bf16[4,256,768]{2,1,0:T(8,128)(2,1)}, u32[]{:S(2)}) copy-start(bf16[4,256,768]{2,1,0:T(8,128)(2,1)} %param.18) | copy-start | bytes 4718596
  429.9 31.2 %copy-start.20 = (f32[1,2,4,128]{3,1,2,0:T(2,128)S(1)}, f32[1,2,4,128]{3,1,2,0:T(2,128)}, u32[]{:S(2)}) copy-start(f32[1,2,4,128]{3,1,2,0:T(2,128)} %copy-done.19) | copy-start | bytes 12292
  429.9 31.2 %copy-start.24 = (f32[768]{0:T(1024)S(1)}, f32[768]{0:T(1024)}, u32[]{:S(2)}) copy-start(f32[768]{0:T(1024)} %copy-done.23) | copy-start | bytes 9220
  429.9 210.8 %reduce-scatter.11.cloned.1.call-start = ((), (), s32[]{:S(2)}) async-start(), calls=%async_computation.13 | async-start | bytes 1990656 | tf_op jit(solution)/shard_map/reduce_scatter | solution.py:278
  432.6 280.7 %reduce-scatter.19.cloned.1.call-start = ((), (), s32[]{:S(2)}) async-start(), calls=%async_computation.17 | async-start | bytes 2654208 | tf_op jit(solution)/shard_map/reduce_scatter | solution.py:280
  457.0 329.1 %reduce-scatter.23.cloned.1.call-start = ((), (), s32[]{:S(2)}) async-start(), calls=%async_computation.19 | async-start | bytes 2654208 | tf_op jit(solution)/shard_map/reduce_scatter | solution.py:281
  461.1 10.3 %copy-start.30 = (f32[1,2,4,128]{3,1,2,0:T(2,128)S(1)}, f32[1,2,4,128]{3,1,2,0:T(2,128)}, u32[]{:S(2)}) copy-start(f32[1,2,4,128]{3,1,2,0:T(2,128)} %copy-done.29) | copy-start | bytes 12292
  471.4 36.0 %copy-start.22 = (f32[1024]{0:T(1024)S(1)}, f32[1024]{0:T(1024)}, u32[]{:S(2)}) copy-start(f32[1024]{0:T(1024)} %copy-done.21) | copy-start | bytes 12292
  471.4 40.6 %copy-start.33 = (f32[768]{0:T(1024)S(1)}, f32[768]{0:T(1024)}, u32[]{:S(2)}) copy-start(f32[768]{0:T(1024)} %copy-done.32) | copy-start | bytes 9220
  (4 other events, 4.5 us)
Sparse Core Ops, SparseCore 0:
  10.9 62.9 all-gather.4
  76.8 52.6 all-gather.6
  132.4 62.4 all-gather.8
  197.7 61.9 all-gather.10
  292.7 23.8 reduce-scatter.12
  364.8 38.6 reduce-scatter.8
  406.1 47.9 reduce-scatter.16
  456.6 47.9 reduce-scatter.20
  508.4 62.6 reduce-scatter.14
  575.1 65.6 reduce-scatter.10
  644.8 68.4 reduce-scatter.18
  717.2 68.8 reduce-scatter.22
where the time goes:
time: 798 us; the launch traced here: 793 us
  waiting for transfers between devices  356 us (45%)
  matrix products  165 us (21%)
  blocking collectives  91.1 us (11%)
  local copies, waits for them, and re-layouts  86.7 us (11%)
  other arithmetic  76 us (10%)
  between operations  17.9 us (2%)
    unnamed x3, blocking collectives  91.1 us
    reduce_scatter x1, waiting for transfers between devices, per_device(): lax.psum_scatter(inner[3], 'wide', scatter_dimension=0, tiled=True)  72.8 us
    reduce_scatter x1, waiting for transfers between devices, per_device(): lax.psum_scatter(inner[2], 'wide', scatter_dimension=0, tiled=True)  72.5 us
    all_gather x1, waiting for transfers between devices, per_device(): lax.all_gather(expand_weight, ('wide', 'narrow'), axis=0, tiled=True)  58.6 us
    reduce_scatter x1, waiting for transfers between devices, per_device(): lax.psum_scatter(inner[0], 'wide', scatter_dimension=0, tiled=True)  53.4 us
    dot_general x4, matrix products, contract_cols(): lax.dot_general(left, right, (((1,), (1,)), ((), ())), preferred_element_...  40.9 us
    dot_general x1, matrix products, per_device(): jnp.dot(second_low, w_expand, preferred_element_type=jnp.float32)  36.6 us
    reduce_scatter x1, waiting for transfers between devices, per_device(): lax.psum_scatter(part_w_reduce.astype(jnp.bfloat16), 'narrow', scatter_di...  33.1 us
  transfers between devices with their start and end apart: 12, of which 8 were waited for; matrix products, arithmetic and copies ran while one was open for 37% of the time, Pallas kernels for 0%

commit v1 on v0

--- a/solution.py
+++ b/solution.py
@@ -6,6 +6,18 @@
 
 HEADS = 12
 HEAD = 64
+
+
+def gather_by_bits(shard, axis, dim):
+    ways, here = (lax.axis_size(axis), lax.axis_index(axis))
+    grown, reach = (shard, 1)
+    while reach < ways:
+        theirs = lax.ppermute(grown, axis, [(d, d ^ reach) for d in range(ways)])
+        mine_first = jnp.concatenate([grown, theirs], axis=dim)
+        theirs_first = jnp.concatenate([theirs, grown], axis=dim)
+        grown = jnp.where(here & reach == 0, mine_first, theirs_first)
+        reach = 2 * reach
+    return grown
 
 
 def layer_norm(inputs, norm_gain, norm_shift):
@@ -62,7 +74,7 @@
         lax.all_gather(input_weight, ("wide", "narrow"), axis=0, tiled=True),
         lax.all_gather(output_weight, ("wide", "narrow"), axis=0, tiled=True),
         lax.all_gather(expand_weight, ("wide", "narrow"), axis=0, tiled=True),
-        lax.all_gather(reduce_weight, ("wide", "narrow"), axis=0, tiled=True),
+        gather_by_bits(reduce_weight, ("wide", "narrow"), 0),
         lax.all_gather(norm1_gain, ("wide", "narrow"), axis=0, tiled=True),
         lax.all_gather(norm1_shift, ("wide", "narrow"), axis=0, tiled=True),
         lax.all_gather(query_bias, ("wide", "narrow"), axis=0, tiled=True),

time: 798 us -> 881 us (1.10)
  waiting for transfers between devices: 356 us -> 422 us
  matrix products: 165 us -> 178 us
    ppermute x0 -> x5, waiting for transfers between devices: none -> 133 us  [gather_by_bits(): theirs = lax.ppermute(grown, axis, [(d, d ^ reach) for d in range(ways)])]
    reduce_scatter x1, waiting for transfers between devices: 33.1 us -> 0.02 us  [per_device(): lax.psum_scatter(part_w_reduce.astype(jnp.bfloat16), 'narrow', scatter_di...]
    reduce_scatter x1, waiting for transfers between devices: 53.4 us -> 23.7 us  [per_device(): lax.psum_scatter(inner[0], 'wide', scatter_dimension=0, tiled=True)]
    dot_general x1, matrix products: 3.53 us -> 13.8 us  [per_device(): jnp.einsum('ihpq,iqhd->iphd', soft_low, values, preferred_element_type=jn...]
    all_gather x1, waiting for transfers between devices: 12.8 us -> 3.54 us  [per_device(): lax.all_gather(output_weight, ('wide', 'narrow'), axis=0, tiled=True)]
    unnamed x122 -> x144, local copies, waits for them, and re-layouts: 26.7 us -> 19 us
  transfers between devices with their start and end apart: 12 -> 17, of which waited for: 8 -> 13; matrix products, arithmetic and copies ran while one was open for 37% -> 34% of each run, Pallas kernels for 0% -> 0%
where the time goes in v1:
time: 881 us; the launch traced here: 876 us
  waiting for transfers between devices  422 us (48%)
  matrix products  178 us (20%)
  blocking collectives  91.4 us (10%)
  other arithmetic  80.6 us (9%)
  local copies, waits for them, and re-layouts  79.2 us (9%)
  between operations  18 us (2%)
    ppermute x5, waiting for transfers between devices, gather_by_bits(): theirs = lax.ppermute(grown, axis, [(d, d ^ reach) for d in range(ways)])  133 us
    unnamed x3, blocking collectives  91.4 us
    reduce_scatter x1, waiting for transfers between devices, per_device(): lax.psum_scatter(inner[3], 'wide', scatter_dimension=0, tiled=True)  72.9 us
    reduce_scatter x1, waiting for transfers between devices, per_device(): lax.psum_scatter(inner[2], 'wide', scatter_dimension=0, tiled=True)  72.6 us
    all_gather x1, waiting for transfers between devices, per_device(): lax.all_gather(expand_weight, ('wide', 'narrow'), axis=0, tiled=True)  58.5 us
    dot_general x4, matrix products, contract_cols(): lax.dot_general(left, right, (((1,), (1,)), ((), ())), preferred_element_...  39.2 us
    dot_general x1, matrix products, per_device(): jnp.dot(second_low, w_expand, preferred_element_type=jnp.float32)  36.6 us
    convert_element_type x1, other arithmetic, per_device(): activated_low = jax.nn.gelu(hidden, approximate=False).astype(jnp.bfloat16)  30 us
  transfers between devices with their start and end apart: 17, of which 13 were waited for; matrix products, arithmetic and copies ran while one was open for 34% of the time, Pallas kernels for 0%

profile of v1, /device:TPU:0, one launch (start us, length us, event | category | flops | bytes accessed | tf_op | source)
XLA Modules:
  0.0 875.7 jit_solution(4514804109947854899)
XLA Ops:
  18.6 43.6 %all-reduce.34 = (bf16[768]{0:T(1024)(128)(2,1)S(1)}, bf16[768]{0:T(1024)(128)(2,1)S(1)}, bf16[768]{0:T(1024)(128)(2,1)S(1)}, bf16[768]{0:T(1024)(128)(2,1)S(1)}...) all-reduce(bf16[768]{0:T(1024)(128)(2,1)S(1)} %dynamic-update-slice, ...), channel_id=1, replica_groups=mesh['wide'=8,'narrow'=4] {'wide','narrow'}, use_global_device_ids=true, to_apply=%add.2 | all-reduce | flops 10752 | bytes 43008
  68.3 5.6 all-gather.5.cloned.1.call-done
  74.0 6.3 fusion.97
  85.0 2.9 reshape.301
  87.9 3.2 copy.121
  91.1 3.9 reshape.302
  97.6 3.9 reshape.300
  101.4 4.5 fusion.23
  106.0 3.8 exponential_reduce_fusion
  110.7 13.8 %fusion.57 = bf16[4,256,12,64]{1,3,2,0:T(8,128)(2,1)S(1)} fusion(bf16[4,256,12,64]{1,0,3,2:T(4,128)(2,1)S(1)} %copy-done.11, f32[4,12,256,256]{2,3,1,0:T(8,128)S(1)} %get-tuple-element.76, f32[4,12,256]{2,1,0:T(8,128)S(1)} %log_add_fusion, pred[4,256]{1,0:T(4,128)(4,1)S(1)} %iota_compare_fusion), kind=kOutput, calls=%fused_computation.108 | convolution fusion | flops 416022528 | bytes 15778816 | tf_op jit(solution)/shard_map/ihpq,iqhd->iphd/dot_general | solution.py:127
  126.2 3.5 all-gather.7.cloned.1.call-done
  129.7 4.6 fusion.93
  136.6 58.5 %all-gather.9.cloned.1.call-done = bf16[768,3072]{1,0:T(8,128)(2,1)} async-done(((bf16[24,3072]{1,0:T(8,128)(2,1)}), bf16[768,3072]{1,0:T(8,128)(2,1)}) %all-gather.9.cloned.1.call-update) | async-done | bytes 4718608 | tf_op jit(solution)/shard_map/all_gather | solution.py:76
  195.1 36.6 %fusion = (f32[1024,3072]{1,0:T(8,128)}, f32[1024,3072]{1,0:T(8,128)}) fusion(f32[3072]{0:T(1024)S(1)} %convert_element_type.344, bf16[768,3072]{1,0:T(8,128)(2,1)} %all-gather.9.cloned.1.call-done, f32[1024,768]{1,0:T(8,128)} %copy-done.8, f32[768]{0:T(1024)S(1)} %convert_element_type.342, f32[768]{0:T(1024)S(1)} %convert_element_type.341, ...), kind=kOutput, calls=%fused_computation.2 | convolution fusion | flops 5033951232 | bytes 33056768 | tf_op jit(solution)/shard_map/dot_general | solution.py:132
  231.7 28.1 %all-gather.11.cloned.1.call-done = bf16[3072,768]{1,0:T(8,128)(2,1)} async-done(((bf16[96,768]{1,0:T(8,128)(2,1)}), bf16[3072,768]{1,0:T(8,128)(2,1)}) %all-gather.11.cloned.1.call-update) | async-done | bytes 4718608 | tf_op jit(solution)/shard_map/all_gather | solution.py:140
  259.8 16.8 %fusion.96 = (bf16[3072]{0:T(1024)(128)(2,1)S(1)}, bf16[1024,3072]{1,0:T(8,128)(2,1)}) fusion(f32[1024,3072]{1,0:T(8,128)} %get-tuple-element.78, bf16[1024,768]{1,0:T(8,128)(2,1)S(1)} %copy-done.15, bf16[3072,768]{1,0:T(8,128)(2,1)} %all-gather.11.cloned.1.call-done, f32[1024,3072]{1,0:T(8,128)} %get-tuple-element.79, f32[3072]{0:T(1024)S(1)} %convert_element_type.344), kind=kOutput, calls=%fused_computation.169 | convolution fusion | flops 4882166784 | bytes 37767168 | tf_op jit(solution)/shard_map/dot_general | solution.py:37
  276.6 9.4 %multiply_reduce_fusion.2 = (bf16[768]{0:T(1024)(128)(2,1)S(1)}, f32[1024]{0:T(1024)S(1)}, bf16[768]{0:T(1024)(128)(2,1)S(1)}, f32[1024,768]{1,0:T(8,128)S(1)}) fusion(f32[1024,768]{1,0:T(8,128)S(1)} %copy-done.9, f32[1024]{0:T(1024)S(1)} %fusion.76, f32[1024]{0:T(1024)S(1)} %broadcast_multiply_fusion, f32[768]{0:T(1024)S(1)} %convert_element_type.341, ...), kind=kOutput, calls=%fused_computation.87 | convolution fusion | flops 4838126592 | bytes 17319936 | tf_op jit(solution)/shard_map/dot_general | solution.py:37
  292.8 3.8 convolution_convert_fusion.4
  296.6 3.1 copy.127
  299.7 3.9 reshape.305
  303.7 11.0 %multiply_reduce_fusion = (f32[4,12,256]{2,1,0:T(8,128)S(1)}, f32[4,12,256,256]{2,3,1,0:T(8,128)}) fusion(f32[4,12,256,256]{2,3,1,0:T(8,128)} %copy-done, f32[4,12,256]{2,1,0:T(8,128)S(1)} %log_add_fusion, pred[4,256]{1,0:T(4,128)(4,1)S(1)} %iota_compare_fusion, bf16[4,256,12,64]{1,0,3,2:T(4,128)(2,1)S(1)} %copy-done.12, bf16[4,256,12,64]{1,0,3,2:T(4,128)(2,1)} %reshape.305), kind=kOutput, calls=%fused_computation.24 | convolution fusion | flops 418369536 | bytes 28410880 | tf_op jit(solution)/shard_map/iphd,iqhd->ihpq/dot_general | solution.py:168
  314.6 13.4 %multiply_convert_fusion = bf16[4,12,256,256]{2,3,1,0:T(8,128)(2,1)} fusion(f32[4,12,256,256]{2,3,1,0:T(8,128)} %get-tuple-element.82, f32[4,12,256,256]{2,3,1,0:T(8,128)} %copy-done, f32[4,12,256]{2,1,0:T(8,128)S(1)} %get-tuple-element.81, f32[4,12,256]{2,1,0:T(8,128)S(1)} %log_add_fusion, pred[4,256]{1,0:T(4,128)(4,1)S(1)} %iota_compare_fusion), kind=kLoop, calls=%fused_computation.23 | loop fusion | flops 18874368 | bytes 31556608 | tf_op jit(solution)/shard_map/convert_element_type | solution.py:176
  328.1 3.4 fusion.95
  336.9 4.8 fusion.60
  344.4 2.8 copy.140
  347.2 4.1 fusion.94
  354.4 6.7 fusion.35
  363.1 9.0 %convolution_convert_fusion = bf16[768,3072]{1,0:T(8,128)(2,1)S(1)} fusion(bf16[1024,3072]{1,0:T(8,128)(2,1)} %get-tuple-element.89, f32[1024,768]{1,0:T(8,128)} %copy-done.8, f32[768]{0:T(1024)S(1)} %convert_element_type.342, f32[768]{0:T(1024)S(1)} %convert_element_type.341, f32[1024]{0:T(1024)S(1)} %fusion.76, f32[1024]{0:T(1024)S(1)} %broadcast_multiply_fusion), kind=kOutput, calls=%fused_computation.50 | convolution fusion | flops 4838129664 | bytes 14170112 | tf_op jit(solution)/shard_map/dot_general | solution.py:31
  375.9 30.0 %fusion.3 = bf16[3072,1024]{0,1:T(8,128)(2,1)} fusion(f32[1024,3072]{1,0:T(8,128)} %get-tuple-element.79, f32[3072]{0:T(1024)S(1)} %convert_element_type.344), kind=kLoop, calls=%fused_computation.5 | loop fusion | flops 207618048 | bytes 18886656 | tf_op jit(solution)/shard_map/convert_element_type | solution.py:133
  406.0 9.0 %copy.146 = bf16[3072,1024]{1,0:T(8,128)(2,1)} copy(bf16[3072,1024]{0,1:T(8,128)(2,1)} %fusion.3) | data formatting | bytes 12582912 | tf_op jit(solution)/shard_map/convert_element_type | solution.py:133
  415.0 8.5 convert_bitcast_fusion
  423.4 2.6 copy.147
  430.7 21.9 %reduce-scatter.17.cloned.1.call-done = bf16[192,3072]{1,0:T(8,128)(2,1)} async-done(((bf16[768,3072]{1,0:T(8,128)(2,1)}), bf16[192,3072]{1,0:T(8,128)(2,1)}) %reduce-scatter.17.cloned.1.call-update) | async-done | bytes 1179664 | tf_op jit(solution)/shard_map/reduce_scatter | solution.py:249
  452.6 2.9 convert_element_type.373
  457.5 8.7 collective-permute-done.1
  467.9 13.1 %collective-permute-done.2 = bf16[384,768]{1,0:T(8,128)(2,1)} collective-permute-done((bf16[384,768]{1,0:T(8,128)(2,1)S(1)}, bf16[384,768]{1,0:T(8,128)(2,1)}, u32[]{:S(2)}, u32[]{:S(2)}) %collective-permute-start.2) | collective-permute-done | bytes 589856 | tf_op jit(solution)/shard_map/ppermute | solution.py:15
  484.5 24.9 %collective-permute-done.3 = bf16[768,768]{1,0:T(8,128)(2,1)} collective-permute-done((bf16[768,768]{1,0:T(8,128)(2,1)S(1)}, bf16[768,768]{1,0:T(8,128)(2,1)}, u32[]{:S(2)}, u32[]{:S(2)}) %collective-permute-start.3) | collective-permute-done | bytes 1179680 | tf_op jit(solution)/shard_map/ppermute | solution.py:15
  509.4 3.2 maximum_select_fusion.2
  519.2 2.8 convert_element_type.380
  522.1 9.1 %fusion.89 = (bf16[768]{0:T(1024)(128)(2,1)S(1)}, f32[1024]{0:T(1024)S(1)}, f32[1024,768]{1,0:T(8,128)}) fusion(f32[768]{0:T(1024)S(1)} %copy-done.24, f32[1024]{0:T(1024)S(1)} %bitcast.243, bf16[4,256,768]{2,1,0:T(8,128)(2,1)S(1)} %copy-done.2, bf16[768,2304]{1,0:T(8,128)(2,1)} %all-gather.5.cloned.1.call-done, bf16[1024,768]{1,0:T(8,128)(2,1)} %copy.141, ...), kind=kOutput, calls=%fused_computation.162 | convolution fusion | flops 3642751232 | bytes 12988928 | tf_op jit(solution)/shard_map/dot_general | solution.py:37
  532.7 3.0 fusion.47
  535.7 84.6 %collective-permute-done.4 = bf16[1536,768]{1,0:T(8,128)(2,1)} collective-permute-done((bf16[1536,768]{1,0:T(8,128)(2,1)}, bf16[1536,768]{1,0:T(8,128)(2,1)}, u32[]{:S(2)}, u32[]{:S(2)}) %collective-permute-start.4) | collective-permute-done | bytes 2359328 | tf_op jit(solution)/shard_map/ppermute | solution.py:15
  620.3 23.8 %multiply_reduce_fusion.1 = (bf16[768]{0:T(1024)(128)(2,1)S(1)}, bf16[768]{0:T(1024)(128)(2,1)S(1)}, f32[1024,768]{1,0:T(8,128)}, bf16[1024,768]{1,0:T(8,128)(2,1)}) fusion(bf16[4,256,768]{2,1,0:T(8,128)(2,1)S(1)} %copy-done.6, f32[1024]{0:T(1024)S(1)} %bitcast.248, f32[768]{0:T(1024)S(1)} %convert_element_type.346, f32[1024,768]{1,0:T(8,128)} %get-tuple-element.77, ...), kind=kOutput, calls=%fused_computation.86 | convolution fusion | flops 4882954240 | bytes 50383872 | tf_op jit(solution)/shard_map/dot_general | solution.py:134
  644.8 10.7 %all-reduce.35 = (bf16[768]{0:T(1024)(128)(2,1)S(1)}, bf16[768]{0:T(1024)(128)(2,1)S(1)}, bf16[768]{0:T(1024)(128)(2,1)S(1)}, bf16[768]{0:T(1024)(128)(2,1)S(1)}...) all-reduce(bf16[768]{0:T(1024)(128)(2,1)S(1)} %convert_element_type, ...), channel_id=10, replica_groups=mesh['wide'=8,'narrow'=4] {'narrow'}, use_global_device_ids=true, to_apply=%region_20.21.clone | all-reduce | flops 10752 | bytes 43008
  655.9 37.1 %all-reduce.33 = (f32[192]{0:T(256)S(1)}, f32[192]{0:T(256)S(1)}, f32[192]{0:T(256)S(1)}, f32[192]{0:T(256)S(1)}, f32[192]{0:T(256)S(1)}, /*index=5*/f32[192]{0:...) all-reduce(f32[192]{0:T(256)S(1)} %get-tuple-element.99, ...), channel_id=11, replica_groups=mesh['wide'=8,'narrow'=4] {'wide'}, use_global_device_ids=true, to_apply=%region_21.22.clone | all-reduce | flops 2688 | bytes 21504
  699.4 23.7 %reduce-scatter.11.cloned.1.call-done = f32[24,2304]{1,0:T(8,128)} async-done(((f32[192,2304]{1,0:T(8,128)}), f32[24,2304]{1,0:T(8,128)}) %reduce-scatter.11.cloned.1.call-update) | async-done | bytes 221200 | tf_op jit(solution)/shard_map/reduce_scatter | solution.py:290
  723.1 72.6 %reduce-scatter.19.cloned.1.call-done = f32[24,3072]{1,0:T(8,128)} async-done(((f32[192,3072]{1,0:T(8,128)}), f32[24,3072]{1,0:T(8,128)}) %reduce-scatter.19.cloned.1.call-update) | async-done | bytes 294928 | tf_op jit(solution)/shard_map/reduce_scatter | solution.py:292
  795.7 72.9 %reduce-scatter.23.cloned.1.call-done = f32[96,768]{1,0:T(8,128)} async-done(((f32[768,768]{1,0:T(8,128)}), f32[96,768]{1,0:T(8,128)}) %reduce-scatter.23.cloned.1.call-update) | async-done | bytes 294928 | tf_op jit(solution)/shard_map/reduce_scatter | solution.py:293
  (270 shorter events, 77.3 us)
Async XLA Ops:
  7.2 55.2 %copy-start.1 = (bf16[4,256,768]{2,1,0:T(8,128)(2,1)S(1)}, bf16[4,256,768]{2,1,0:T(8,128)(2,1)}, u32[]{:S(2)}) copy-start(bf16[4,256,768]{2,1,0:T(8,128)(2,1)} %param.18) | copy-start | bytes 4718596
  7.2 9.5 %copy-start.38 = (bf16[24]{0:T(256)(128)(2,1)S(1)}, bf16[24]{0:T(256)(128)(2,1)}, u32[]{:S(2)}) copy-start(bf16[24]{0:T(256)(128)(2,1)} %param.30) | copy-start | bytes 148
  7.2 9.7 %copy-start.39 = (bf16[24]{0:T(256)(128)(2,1)S(1)}, bf16[24]{0:T(256)(128)(2,1)}, u32[]{:S(2)}) copy-start(bf16[24]{0:T(256)(128)(2,1)} %param.29) | copy-start | bytes 148
  7.3 9.9 %copy-start.40 = (bf16[24]{0:T(256)(128)(2,1)S(1)}, bf16[24]{0:T(256)(128)(2,1)}, u32[]{:S(2)}) copy-start(bf16[24]{0:T(256)(128)(2,1)} %param.27) | copy-start | bytes 148
  7.3 10.2 %copy-start.41 = (bf16[24]{0:T(256)(128)(2,1)S(1)}, bf16[24]{0:T(256)(128)(2,1)}, u32[]{:S(2)}) copy-start(bf16[24]{0:T(256)(128)(2,1)} %param.28) | copy-start | bytes 148
  7.3 10.4 %copy-start.42 = (bf16[24]{0:T(256)(128)(2,1)S(1)}, bf16[24]{0:T(256)(128)(2,1)}, u32[]{:S(2)}) copy-start(bf16[24]{0:T(256)(128)(2,1)} %param.25) | copy-start | bytes 148
  7.3 10.6 %copy-start.43 = (bf16[24]{0:T(256)(128)(2,1)S(1)}, bf16[24]{0:T(256)(128)(2,1)}, u32[]{:S(2)}) copy-start(bf16[24]{0:T(256)(128)(2,1)} %param.26) | copy-start | bytes 148
  7.3 10.8 %copy-start.44 = (bf16[24]{0:T(256)(128)(2,1)S(1)}, bf16[24]{0:T(256)(128)(2,1)}, u32[]{:S(2)}) copy-start(bf16[24]{0:T(256)(128)(2,1)} %param.35) | copy-start | bytes 148
  7.3 11.1 %copy-start.45 = (bf16[96]{0:T(256)(128)(2,1)S(1)}, bf16[96]{0:T(256)(128)(2,1)}, u32[]{:S(2)}) copy-start(bf16[96]{0:T(256)(128)(2,1)} %param.33) | copy-start | bytes 580
  7.3 66.6 %all-gather.5.cloned.1.call-start = ((), (), s32[]{:S(2)}) async-start(), calls=%async_computation.8 | async-start | bytes 3649536 | tf_op jit(solution)/shard_map/all_gather | solution.py:74
  8.1 121.6 %all-gather.7.cloned.1.call-start = ((), (), s32[]{:S(2)}) async-start(), calls=%async_computation.9 | async-start | bytes 1216512 | tf_op jit(solution)/shard_map/all_gather | solution.py:75
  8.8 186.3 %all-gather.9.cloned.1.call-start = ((), (), s32[]{:S(2)}) async-start(), calls=%async_computation.10 | async-start | bytes 4866048 | tf_op jit(solution)/shard_map/all_gather | solution.py:76
  9.5 250.2 %all-gather.11.cloned.1.call-start = ((), (), s32[]{:S(2)}) async-start(), calls=%async_computation.11 | async-start | bytes 4866048 | tf_op jit(solution)/shard_map/all_gather | solution.py:140
  10.1 416.0 %reduce-scatter.13.cloned.1.call-start = ((), (), s32[]{:S(2)}) async-start(), calls=%async_computation.14 | async-start | bytes 1474560 | tf_op jit(solution)/shard_map/reduce_scatter | solution.py:246
  13.9 52.8 %copy-start.19 = (f32[1,2,4,128]{3,1,2,0:T(2,128)}, f32[1,2,4,128]{3,1,2,0:T(2,128)S(1)}, u32[]{:S(2)}) copy-start(f32[1,2,4,128]{3,1,2,0:T(2,128)S(1)} %copy.166) | copy-start | bytes 12292
  15.9 50.8 %copy-start.5 = (bf16[4,256,768]{2,1,0:T(8,128)(2,1)S(1)}, bf16[4,256,768]{2,1,0:T(8,128)(2,1)}, u32[]{:S(2)}) copy-start(bf16[4,256,768]{2,1,0:T(8,128)(2,1)} %param.20) | copy-start | bytes 4718596
  16.0 46.3 %copy-start.29 = (f32[1,2,4,128]{3,1,2,0:T(2,128)}, f32[1,2,4,128]{3,1,2,0:T(2,128)S(1)}, u32[]{:S(2)}) copy-start(f32[1,2,4,128]{3,1,2,0:T(2,128)S(1)} %copy.167) | copy-start | bytes 12292
  16.0 52.4 %copy-start.21 = (f32[1024]{0:T(1024)}, f32[1024]{0:T(1024)S(1)}, u32[]{:S(2)}) copy-start(f32[1024]{0:T(1024)S(1)} %rsqrt.22) | copy-start | bytes 12292
  62.3 67.4 %copy-start.32 = (f32[768]{0:T(1024)}, f32[768]{0:T(1024)S(1)}, u32[]{:S(2)}) copy-start(f32[768]{0:T(1024)S(1)} %convert_element_type.339) | copy-start | bytes 9220
  87.9 13.5 %copy-start.3 = (bf16[4,256,12,64]{1,0,3,2:T(4,128)(2,1)}, bf16[4,256,12,64]{1,0,3,2:T(4,128)(2,1)S(1)}, u32[]{:S(2)}) copy-start(bf16[4,256,12,64]{1,0,3,2:T(4,128)(2,1)S(1)} %reshape.301) | copy-start | bytes 4718596
  136.6 123.2 %copy-start.15 = (bf16[1024,768]{1,0:T(8,128)(2,1)S(1)}, bf16[1024,768]{1,0:T(8,128)(2,1)}, u32[]{:S(2)}) copy-start(bf16[1024,768]{1,0:T(8,128)(2,1)} %multiply_convert_fusion.7) | copy-start | bytes 4718596
  259.8 16.9 %copy-start.9 = (f32[1024,768]{1,0:T(8,128)S(1)}, f32[1024,768]{1,0:T(8,128)}, u32[]{:S(2)}) copy-start(f32[1024,768]{1,0:T(8,128)} %copy-done.8) | copy-start | bytes 9437188
  292.8 135.3 %reduce-scatter.9.cloned.1.call-start = ((), (), s32[]{:S(2)}) async-start(), calls=%async_computation.12 | async-start | bytes 4423680 | tf_op jit(solution)/shard_map/reduce_scatter | solution.py:243
  303.7 24.4 %slice-start = ((s8[12582912]{0:T(1024)(128)(4,1)}), s8[4194304]{0:T(1024)(128)(4,1)S(1)}, s32[]{:S(2)}) async-start(s8[12582912]{0:T(1024)(128)(4,1)} %bitcast.222), calls=%async_computation.20 | async-start | bytes 8388608
  303.7 24.4 %slice-start.1 = ((s8[12582912]{0:T(1024)(128)(4,1)}), s8[4194304]{0:T(1024)(128)(4,1)S(1)}, s32[]{:S(2)}) async-start(s8[12582912]{0:T(1024)(128)(4,1)} %bitcast.222), calls=%async_computation.21 | async-start | bytes 8388608
  314.6 13.4 %slice-start.2 = ((s8[12582912]{0:T(1024)(128)(4,1)}), s8[4194304]{0:T(1024)(128)(4,1)S(1)}, s32[]{:S(2)}) async-start(s8[12582912]{0:T(1024)(128)(4,1)} %bitcast.222), calls=%async_computation.22 | async-start | bytes 8388608
  314.6 13.4 %copy-start.13 = (bf16[4,256,12,64]{1,0,3,2:T(4,128)(2,1)S(1)}, bf16[4,256,12,64]{1,0,3,2:T(4,128)(2,1)}, u32[]{:S(2)}) copy-start(bf16[4,256,12,64]{1,0,3,2:T(4,128)(2,1)} %reshape.305) | copy-start | bytes 4718596
  363.1 89.5 %reduce-scatter.17.cloned.1.call-start = ((), (), s32[]{:S(2)}) async-start(), calls=%async_computation.16 | async-start | bytes 5898240 | tf_op jit(solution)/shard_map/reduce_scatter | solution.py:249
  374.7 144.5 %reduce-scatter.21.cloned.1.call-start = ((), (), s32[]{:S(2)}) async-start(), calls=%async_computation.18 | async-start | bytes 5898240 | tf_op jit(solution)/shard_map/reduce_scatter | solution.py:252
  426.1 273.4 %reduce-scatter.15.cloned.1.call-start = ((), (), s32[]{:S(2)}) async-start(), calls=%async_computation.15 | async-start | bytes 663552 | tf_op jit(solution)/shard_map/reduce_scatter | solution.py:291
  428.0 295.1 %reduce-scatter.11.cloned.1.call-start = ((), (), s32[]{:S(2)}) async-start(), calls=%async_computation.13 | async-start | bytes 1990656 | tf_op jit(solution)/shard_map/reduce_scatter | solution.py:290
  430.6 25.0 %copy-start.18 = (bf16[96,768]{1,0:T(8,128)(2,1)S(1)}, bf16[96,768]{1,0:T(8,128)(2,1)}, u32[]{:S(2)}) copy-start(bf16[96,768]{1,0:T(8,128)(2,1)} %param.24) | copy-start | bytes 442372
  430.6 365.1 %reduce-scatter.19.cloned.1.call-start = ((), (), s32[]{:S(2)}) async-start(), calls=%async_computation.17 | async-start | bytes 2654208 | tf_op jit(solution)/shard_map/reduce_scatter | solution.py:292
  455.5 413.1 %reduce-scatter.23.cloned.1.call-start = ((), (), s32[]{:S(2)}) async-start(), calls=%async_computation.19 | async-start | bytes 2654208 | tf_op jit(solution)/shard_map/reduce_scatter | solution.py:293
  455.6 1.4 collective-permute-start
  457.1 9.1 %collective-permute-start.1 = (bf16[192,768]{1,0:T(8,128)(2,1)S(1)}, bf16[192,768]{1,0:T(8,128)(2,1)S(1)}, u32[]{:S(2)}, u32[]{:S(2)}) collective-permute-start(bf16[192,768]{1,0:T(8,128)(2,1)S(1)} %maximum_select_fusion.5), channel_id=1, source_target_pairs={{0,2},{1,3},{2,0},{3,1},{4,6},{5,7},{6,4},{7,5},{8,10},{9,11},{10,... | collective-permute-start | bytes 884744 | tf_op jit(solution)/shard_map/ppermute | solution.py:15
  466.4 14.7 %collective-permute-start.2 = (bf16[384,768]{1,0:T(8,128)(2,1)S(1)}, bf16[384,768]{1,0:T(8,128)(2,1)}, u32[]{:S(2)}, u32[]{:S(2)}) collective-permute-start(bf16[384,768]{1,0:T(8,128)(2,1)S(1)} %maximum_select_fusion.4), channel_id=1, source_target_pairs={{0,4},{1,5},{2,6},{3,7},{4,0},{5,1},{6,2},{7,3},{8,12},{9,13},{10,... | collective-permute-start | bytes 1769480 | tf_op jit(solution)/shard_map/ppermute | solution.py:15
  467.9 47.2 %copy-start.47 = (u32[32]{0:T(128)S(1)}, u32[32]{0:T(128)}, u32[]{:S(2)}) copy-start(u32[32]{0:T(128)} %constant.180) | copy-start | bytes 388
  467.9 49.1 %copy-start.46 = (u32[32]{0:T(128)S(1)}, u32[32]{0:T(128)}, u32[]{:S(2)}) copy-start(u32[32]{0:T(128)} %constant.176) | copy-start | bytes 388
  467.9 51.0 %copy-start.34 = (bf16[768]{0:T(1024)(128)(2,1)S(1)}, bf16[768]{0:T(1024)(128)(2,1)}, u32[]{:S(2)}) copy-start(bf16[768]{0:T(1024)(128)(2,1)} %get-tuple-element.46) | copy-start | bytes 4612
  483.0 26.5 %collective-permute-start.3 = (bf16[768,768]{1,0:T(8,128)(2,1)S(1)}, bf16[768,768]{1,0:T(8,128)(2,1)}, u32[]{:S(2)}, u32[]{:S(2)}) collective-permute-start(bf16[768,768]{1,0:T(8,128)(2,1)S(1)} %maximum_select_fusion.3), channel_id=1, source_target_pairs={{0,8},{1,9},{2,10},{3,11},{4,12},{5,13},{6,14},{7,15},{8,0},{9,1},... | collective-permute-start | bytes 3538952 | tf_op jit(solution)/shard_map/ppermute | solution.py:15
  512.7 9.4 %copy-start.2 = (bf16[4,256,768]{2,1,0:T(8,128)(2,1)S(1)}, bf16[4,256,768]{2,1,0:T(8,128)(2,1)}, u32[]{:S(2)}) copy-start(bf16[4,256,768]{2,1,0:T(8,128)(2,1)} %param.18) | copy-start | bytes 4718596
  512.7 9.4 %copy-start.20 = (f32[1,2,4,128]{3,1,2,0:T(2,128)S(1)}, f32[1,2,4,128]{3,1,2,0:T(2,128)}, u32[]{:S(2)}) copy-start(f32[1,2,4,128]{3,1,2,0:T(2,128)} %copy-done.19) | copy-start | bytes 12292
  512.7 9.4 %copy-start.24 = (f32[768]{0:T(1024)S(1)}, f32[768]{0:T(1024)}, u32[]{:S(2)}) copy-start(f32[768]{0:T(1024)} %copy-done.23) | copy-start | bytes 9220
  512.7 107.7 %collective-permute-start.4 = (bf16[1536,768]{1,0:T(8,128)(2,1)}, bf16[1536,768]{1,0:T(8,128)(2,1)}, u32[]{:S(2)}, u32[]{:S(2)}) collective-permute-start(bf16[1536,768]{1,0:T(8,128)(2,1)} %maximum_select_fusion.2), channel_id=1, source_target_pairs={{0,16},{1,17},{2,18},{3,19},{4,20},{5,21},{6,22},{7,23},{8,24},{9,... | collective-permute-start | bytes 7077896 | tf_op jit(solution)/shard_map/ppermute | solution.py:15
  522.1 10.6 %copy-start.30 = (f32[1,2,4,128]{3,1,2,0:T(2,128)S(1)}, f32[1,2,4,128]{3,1,2,0:T(2,128)}, u32[]{:S(2)}) copy-start(f32[1,2,4,128]{3,1,2,0:T(2,128)} %copy-done.29) | copy-start | bytes 12292
  522.1 10.6 %copy-start.22 = (f32[1024]{0:T(1024)S(1)}, f32[1024]{0:T(1024)}, u32[]{:S(2)}) copy-start(f32[1024]{0:T(1024)} %copy-done.21) | copy-start | bytes 12292
  531.3 89.1 %copy-start.33 = (f32[768]{0:T(1024)S(1)}, f32[768]{0:T(1024)}, u32[]{:S(2)}) copy-start(f32[768]{0:T(1024)} %copy-done.32) | copy-start | bytes 9220
  (20 other events, 92.6 us)
Sparse Core Ops, SparseCore 0:
  11.0 62.8 all-gather.4
  76.9 52.7 all-gather.6
  132.6 62.4 all-gather.8
  197.9 61.8 all-gather.10
  292.9 23.8 reduce-scatter.12
  363.2 38.8 reduce-scatter.8
  404.6 47.9 reduce-scatter.16
  455.1 47.9 reduce-scatter.20
  507.0 146.5 reduce-scatter.14
  657.4 65.6 reduce-scatter.10
  727.2 68.4 reduce-scatter.18
  799.6 68.9 reduce-scatter.22
